TPU v7x, 32 devices: a whole 2x2x4 slice. The times are simulated.
32 devices in a mesh: seg: 8 (over z, x), sub: 4 (over y, core).
Axes of the slice: x: 2, y: 2, z: 4, core: 2. Of those that a mesh axis runs over, the one named last changes fastest.
Arguments:
- leaf_mult: float32 [32768, 256], P(('seg', 'sub')), may hold values from -6 to 6
- m2m_ops: float32 [8, 256, 256], replicated, may hold values from -0.125 to 0.125
- m2l_ops: float32 [32, 256, 256], replicated, may hold values from -0.0625 to 0.0625
- owner_box: int32 [4096], P(('seg', 'sub')), may hold values from 0 to 4095, as said below
- src_list: int32 [4096, 32], P(('seg', 'sub')), may hold values from -1 to 4095, as said below
Outputs:
- parent_mult: float32 [4096, 256], P(('seg', 'sub'))
- owned_mult: float32 [4096, 256], P(('seg', 'sub'))
- local_exp: float32 [4096, 256], P(('seg', 'sub'))
Inputs may be any that keep to these rules, and one draw needn't show every extreme that they name: `owner_box`: each aligned block of 512 rows, the g-th, holds every box id from g * 512 to (g + 1) * 512 - 1 once. `src_list`: A slot of a row in the g-th aligned block of 512 rows is -1 or names a box of the blocks g - 1, g or g + 1 of Morton order, each block being 512 consecutive ids.
All inputs are finite; a program needn't handle non-finite values.
Results may differ from a plain program's by a relative error of at most 0.000082.
Values sent between devices are 32-bit elements; how exact they have to be, the bound alone decides.
A program may use at most 64 MiB of HBM per device.

v0:
```python
import jax
import jax.numpy as jnp
from jax import lax
from jax.sharding import PartitionSpec as P


def extended(block, sides, width):
    for axis, dim in sides:
        count = lax.axis_size(axis)
        forward = [(i, i + 1) for i in range(count - 1)]
        backward = [(target, source) for source, target in forward]
        low = lax.ppermute(
            lax.slice_in_dim(block, block.shape[dim] - width, None, axis=dim), axis, forward
        )
        high = lax.ppermute(lax.slice_in_dim(block, 0, width, axis=dim), axis, backward)
        block = jnp.concatenate([low, block, high], axis=dim)
    return block


def on_device(leaf_mult, m2m_ops, m2l_ops, owner_box, src_list):
    per_dev = leaf_mult.shape[0] // 8
    coef_width = leaf_mult.shape[1]
    children = leaf_mult.reshape(per_dev, 8, coef_width)
    parent_mult = jnp.einsum("pck,ckl->pl", children, m2m_ops, precision=lax.Precision.HIGHEST)
    group_rows = per_dev * lax.axis_size("sub")
    window_start = (lax.axis_index("seg") - 1) * group_rows
    gathered = lax.all_gather(parent_mult, "sub", axis=0, tiled=True)
    window = extended(gathered, (("seg", 0),), group_rows)

    def locate(box_ids):
        return box_ids - window_start

    owned_mult = jnp.take(window, locate(owner_box), axis=0)
    present = src_list >= 0
    clamped = jnp.where(present, src_list, window_start + group_rows)
    slot_rows = locate(clamped).T
    sources = jnp.take(window, slot_rows, axis=0)
    sources = jnp.where(present.T[:, :, None], sources, jnp.float32(0.0))
    local_exp = jnp.einsum("jrk,jkl->rl", sources, m2l_ops, precision=lax.Precision.HIGHEST)
    return (parent_mult, owned_mult, local_exp)


def solution(mesh):
    in_specs = (P(("seg", "sub"), None), P(), P(), P(("seg", "sub")), P(("seg", "sub"), None))
    out_specs = (P(("seg", "sub"), None), P(("seg", "sub"), None), P(("seg", "sub"), None))
    return jax.shard_map(
        on_device, mesh=mesh, in_specs=in_specs, out_specs=out_specs, check_vma=False
    )
```

profile of v0, /device:TPU:0, one launch (start us, length us, event | category | flops | bytes accessed | tf_op | source)
XLA Modules:
  0.0 72.2 jit_solution(10723563132042959471)
XLA Ops:
  0.6 0.0 copy-start
  0.6 1.6 %copy-done = f32[8,256,256]{2,1,0:T(8,128)S(1)} copy-done((f32[8,256,256]{2,1,0:T(8,128)S(1)}, f32[8,256,256]{2,1,0:T(8,128)}, u32[]{:S(2)}) %copy-start) | copy-done | bytes 2097176
  2.2 2.5 %convolution_bitcast_fusion = f32[128,256]{1,0:T(8,128)S(1)} fusion(f32[8,256,256]{2,1,0:T(8,128)S(1)} %copy-done, f32[128,8,256]{2,1,0:T(8,128)} %bitcast.21), kind=kOutput, calls=%fused_computation.10 | convolution fusion | flops 805306368 | bytes 3276800 | tf_op jit(solution)/shard_map/pck,ckl->pl/dot_general | solution.py:24
  4.7 0.0 copy-start.1
  4.7 8.7 %all_gather.3 = f32[512,256]{1,0:T(8,128)S(1)} all-gather(f32[128,256]{1,0:T(8,128)S(1)} %convolution_bitcast_fusion), channel_id=1, replica_groups=mesh['seg'=8,'sub'=4] {'sub'}, dimensions={0}, use_global_device_ids=true | all-gather | bytes 655360 | tf_op jit(solution)/shard_map/all_gather | solution.py:27
  13.4 4.2 %collective-permute-start = (f32[512,256]{1,0:T(8,128)S(1)}, f32[512,256]{1,0:T(8,128)}, u32[]{:S(2)}, u32[]{:S(2)}) collective-permute-start(f32[512,256]{1,0:T(8,128)S(1)} %all_gather.3), channel_id=1, source_target_pairs={{0,4},{4,8},{8,12},{12,16},{16,20},{20,24},{24,28},{1,5},{5,9},{9,... | collective-permute-start | bytes 1572872 | tf_op jit(solution)/shard_map/ppermute | solution.py:12
  17.6 1.3 %collective-permute-start.1 = (f32[512,256]{1,0:T(8,128)S(1)}, f32[512,256]{1,0:T(8,128)S(1)}, u32[]{:S(2)}, u32[]{:S(2)}) collective-permute-start(f32[512,256]{1,0:T(8,128)S(1)} %all_gather.3), channel_id=1, source_target_pairs={{4,0},{8,4},{12,8},{16,12},{20,16},{24,20},{28,24},{5,1},{9,5},{13... | collective-permute-start | bytes 1572872 | tf_op jit(solution)/shard_map/ppermute | solution.py:15
  18.9 0.7 %compare_bitcast_fusion = pred[32,128]{1,0:T(8,128)(4,1)S(1)} fusion(s32[128,32]{0,1:T(8,128)} %param.9), kind=kLoop, calls=%fused_computation.15 | loop fusion | flops 4096 | bytes 20480 | tf_op jit(solution)/shard_map/transpose | solution.py:38
  19.6 0.7 %compare_and_fusion = pred[32,128]{1,0:T(8,128)(4,1)S(1)} fusion(s32[128,32]{0,1:T(8,128)} %param.9, s32[]{:T(128)S(6)} %mul.3, s32[]{:T(128)S(6)} %add.22), kind=kLoop, calls=%fused_computation.19 | loop fusion | flops 36864 | bytes 20488 | tf_op jit(solution)/shard_map/jit(_take)/and | solution.py:37
  20.4 0.7 compare_and_fusion.1
  21.0 0.7 %bitcast_clamp_fusion = s32[4096]{0:T(1024)S(1)} fusion(s32[128,32]{0,1:T(8,128)} %param.9, s32[]{:T(128)S(6)} %mul.3, s32[]{:T(128)S(6)} %add.22), kind=kLoop, calls=%fused_computation.18 | loop fusion | flops 28672 | bytes 32776 | tf_op jit(solution)/shard_map/jit(_take)/gather | solution.py:37
  21.8 18.0 %collective-permute-done = f32[512,256]{1,0:T(8,128)} collective-permute-done((f32[512,256]{1,0:T(8,128)S(1)}, f32[512,256]{1,0:T(8,128)}, u32[]{:S(2)}, u32[]{:S(2)}) %collective-permute-start) | collective-permute-done | bytes 524320 | tf_op jit(solution)/shard_map/ppermute | solution.py:12
  39.7 1.9 %constant_dynamic-update-slice_fusion.2 = f32[1536,256]{1,0:T(8,128)} fusion(f32[512,256]{1,0:T(8,128)} %collective-permute-done), kind=kLoop, calls=%fused_computation.22 | loop fusion | bytes 1048576
  41.6 0.8 %constant_dynamic-update-slice_fusion.1 = f32[1536,256]{1,0:T(8,128)} fusion(f32[1536,256]{1,0:T(8,128)} %constant_dynamic-update-slice_fusion.2, f32[512,256]{1,0:T(8,128)S(1)} %all_gather.3), kind=kLoop, calls=%fused_computation.21 | loop fusion | bytes 1048576
  42.5 0.0 collective-permute-done.1
  42.5 0.8 %constant_dynamic-update-slice_fusion = f32[1536,256]{1,0:T(8,128)} fusion(f32[1536,256]{1,0:T(8,128)} %constant_dynamic-update-slice_fusion.1, f32[512,256]{1,0:T(8,128)S(1)} %collective-permute-done.1), kind=kLoop, calls=%fused_computation.20 | loop fusion | bytes 1048576 | tf_op jit(solution)/shard_map/concatenate | solution.py:16
  43.3 17.5 %gather_fusion.1 = f32[4096,256]{1,0:T(8,128)} fusion(f32[1536,256]{1,0:T(8,128)} %constant_dynamic-update-slice_fusion, s32[4096]{0:T(1024)S(1)} %bitcast_clamp_fusion), kind=kCustom, calls=%fused_computation.1 | custom fusion | bytes 8404992 | tf_op jit(solution)/shard_map/jit(_take)/gather | solution.py:37
  60.8 0.0 copy-done.1
  60.9 2.2 %gather_fusion = f32[128,256]{1,0:T(8,128)S(1)} fusion(f32[1536,256]{1,0:T(8,128)} %constant_dynamic-update-slice_fusion, s32[1024]{0:T(1024)S(1)} %pad_clamp_fusion), kind=kCustom, calls=%fused_computation | custom fusion | bytes 262656 | tf_op jit(solution)/shard_map/jit(_take)/gather | solution.py:33
  63.0 0.7 %broadcast_select_fusion = f32[128,256]{1,0:T(8,128)} fusion(f32[128,256]{1,0:T(8,128)S(1)} %gather_fusion, pred[128]{0:T(512)(128)(4,1)S(1)} %get-tuple-element.3), kind=kLoop, calls=%fused_computation.12 | loop fusion | flops 32768 | bytes 262272 | tf_op jit(solution)/shard_map/jit(_take)/select_n | solution.py:33
  63.8 8.5 %fusion.7 = f32[128,256]{1,0:T(8,128)} fusion(f32[32,256,256]{2,1,0:T(8,128)} %param.7, f32[32,128,256]{2,1,0:T(8,128)} %bitcast.20, pred[32,128]{1,0:T(8,128)(4,1)S(1)} %compare_and_fusion, pred[32,128]{1,0:T(8,128)(4,1)S(1)} %compare_bitcast_fusion), kind=kOutput, calls=%fused_computation.9 | convolution fusion | flops 3223322624 | bytes 12722176 | tf_op jit(solution)/shard_map/jrk,jkl->rl/dot_general | solution.py:39
  (1 shorter events, 0.0 us)
Async XLA Ops:
  0.6 1.6 %copy-start = (f32[8,256,256]{2,1,0:T(8,128)S(1)}, f32[8,256,256]{2,1,0:T(8,128)}, u32[]{:S(2)}) copy-start(f32[8,256,256]{2,1,0:T(8,128)} %param.6) | copy-start | bytes 6291460
  4.7 56.1 %copy-start.1 = (f32[128,256]{1,0:T(8,128)}, f32[128,256]{1,0:T(8,128)S(1)}, u32[]{:S(2)}) copy-start(f32[128,256]{1,0:T(8,128)S(1)} %convolution_bitcast_fusion) | copy-start | bytes 393220
  13.4 26.3 %collective-permute-start = (f32[512,256]{1,0:T(8,128)S(1)}, f32[512,256]{1,0:T(8,128)}, u32[]{:S(2)}, u32[]{:S(2)}) collective-permute-start(f32[512,256]{1,0:T(8,128)S(1)} %all_gather.3), channel_id=1, source_target_pairs={{0,4},{4,8},{8,12},{12,16},{16,20},{20,24},{24,28},{1,5},{5,9},{9,... | collective-permute-start | bytes 1572872 | tf_op jit(solution)/shard_map/ppermute | solution.py:12
  17.6 24.9 %collective-permute-start.1 = (f32[512,256]{1,0:T(8,128)S(1)}, f32[512,256]{1,0:T(8,128)S(1)}, u32[]{:S(2)}, u32[]{:S(2)}) collective-permute-start(f32[512,256]{1,0:T(8,128)S(1)} %all_gather.3), channel_id=1, source_target_pairs={{4,0},{8,4},{12,8},{16,12},{20,16},{24,20},{28,24},{5,1},{9,5},{13... | collective-permute-start | bytes 1572872 | tf_op jit(solution)/shard_map/ppermute | solution.py:15
where the time goes:
time: 72.8 us; the launch traced here: 72.2 us
  local copies, waits for them, and re-layouts  24.9 us (34%)
  waiting for transfers between devices  18 us (25%)
  matrix products  11 us (15%)
  blocking collectives  8.68 us (12%)
  starting transfers between devices  5.47 us (8%)
  other arithmetic  3.6 us (5%)
    ppermute x1, waiting for transfers between devices, extended(): lax.ppermute(lax.slice_in_dim(block, block.shape[dim] - width, None, axis...  18 us
    gather x1, local copies, waits for them, and re-layouts, on_device(): sources = jnp.take(window, slot_rows, axis=0)  17.5 us
    all_gather x1, blocking collectives, on_device(): gathered = lax.all_gather(parent_mult, 'sub', axis=0, tiled=True)  8.68 us
    dot_general x1, matrix products, on_device(): jnp.einsum('jrk,jkl->rl', sources, m2l_ops, precision=lax.Precision.HIGHEST)  8.48 us
    unnamed x6, local copies, waits for them, and re-layouts  4.34 us
    ppermute x1, starting transfers between devices, extended(): lax.ppermute(lax.slice_in_dim(block, block.shape[dim] - width, None, axis...  4.19 us
    dot_general x1, matrix products, on_device(): jnp.einsum('pck,ckl->pl', children, m2m_ops, precision=lax.Precision.HIGH...  2.5 us
    gather x1, local copies, waits for them, and re-layouts, on_device(): owned_mult = jnp.take(window, locate(owner_box), axis=0)  2.16 us
  transfers between devices with their start and end apart: 2, of which 1 were waited for; matrix products, arithmetic and copies ran while one was open for 8% of the time, Pallas kernels for 0%

commit v1 on v0

v1 whole, which is shorter than its diff:
```python
import functools

import jax
import jax.numpy as jnp
from jax import lax
from jax.experimental import pallas as pl
from jax.experimental.pallas import tpu as pltpu
from jax.sharding import PartitionSpec as P

MESH = pl.DeviceIdType.MESH
LANES = 128
BATCH = 4


def split(value):
    high = value.astype(jnp.bfloat16)
    low = (value - high.astype(jnp.float32)).astype(jnp.bfloat16)
    return high, low


def kernel(
    n_seg, n_sub, parent, src_t, owner, ops_hbm, owned_out, local_out,
    pair, far, pair_parts, far_parts, ops, ops_high, ops_low, index, picked,
    ops_sem, own_sem, send_sem, recv_sem,
):
    seg, sub = lax.axis_index("seg"), lax.axis_index("sub")
    rows, width = parent.shape
    slots = src_t.shape[0]
    n_high = n_sub // 2
    side, core, high = seg % 2, sub % 2, sub // 2
    partner = seg + 1 - 2 * side
    other_side = 1 - side
    sibling = sub + 1 - 2 * core
    target = seg + 2 - 4 * side
    origin = seg - 2 + 4 * side
    has_target = (target >= 0) & (target < n_seg)
    has_origin = (origin >= 0) & (origin < n_seg)
    half = rows // 2
    group_rows = rows * n_sub

    ops_copy = pltpu.make_async_copy(ops_hbm, ops, ops_sem)
    ops_copy.start()

    barrier = pltpu.get_barrier_semaphore()

    def greet(to_seg, to_sub):
        pl.semaphore_signal(barrier, inc=1, device_id=(to_seg, to_sub), device_id_type=MESH)

    def peer(step):
        return lax.rem(high + step, n_high) * 2 + core

    greet(seg, sibling)
    greet(partner, sub)
    for step in range(1, n_high):
        greet(seg, peer(step))

    @pl.when(has_target)
    def _():
        greet(target, sub)

    @pl.when(has_origin)
    def _():
        greet(origin, sub)

    pl.semaphore_wait(barrier, 1 + n_high + has_target.astype(jnp.int32) + has_origin.astype(jnp.int32))

    names = {}

    def copy(name, src, dst, to_seg, to_sub):
        k = names.setdefault(name, len(names))
        return pltpu.make_async_remote_copy(
            src_ref=src, dst_ref=dst, send_sem=send_sem.at[k], recv_sem=recv_sem.at[k],
            device_id=(to_seg, to_sub), device_id_type=MESH,
        )

    def piece(part):
        return pl.ds(part * half, half)

    sent = []

    def go(c):
        c.start()
        sent.append(c)
        return c

    def to_x(part):
        return copy(("x", part), parent.at[piece(part)], pair.at[side, sub, piece(part)], partner, sub)

    def from_x(part):
        return copy(("x", part), parent.at[piece(part)], pair.at[other_side, sub, piece(part)], partner, sub)

    def to_y(step, part):
        return copy(("y", step, part), parent.at[piece(part)], pair.at[side, sub, piece(part)], seg, peer(step))

    def from_y(step, part):
        at = pair.at[side, peer(n_high - step), piece(part)]
        return copy(("y", step, part), parent.at[piece(part)], at, seg, peer(step))

    def xy(step):
        at = pair.at[other_side, sub, piece(0)]
        return copy(("xy", step), at, at, seg, peer(step))

    def from_xy(step):
        at = pair.at[other_side, peer(n_high - step), piece(0)]
        return copy(("xy", step), at, at, seg, peer(step))

    def yx(step):
        at = pair.at[side, peer(step), piece(1)]
        return copy(("yx", step), at, at, partner, sub)

    def from_yx(step):
        at = pair.at[other_side, peer(step), piece(1)]
        return copy(("yx", step), at, at, partner, sub)

    def z(step, part):
        return copy(
            ("z", step, part), pair.at[other_side, peer(step), piece(part)],
            far.at[peer(step), piece(part)], target, sub,
        )

    def to_sibling(step, which):
        at = far.at[peer(step)] if which == 2 else pair.at[(side, other_side)[which], peer(step)]
        src = parent if (step, which) == (0, 0) else at
        return copy(("s", step, which), src, at, seg, sibling)

    def from_sibling(step, which):
        s = lax.rem(high + step, n_high) * 2 + 1 - core
        at = far.at[s] if which == 2 else pair.at[(side, other_side)[which], s]
        return copy(("s", step, which), at, at, seg, sibling)

    go(to_x(0))
    for step in range(1, n_high):
        go(to_y(step, 1))
    go(to_x(1))
    for step in range(1, n_high):
        go(to_y(step, 0))
    go(to_sibling(0, 0))
    own = pltpu.make_async_copy(parent, pair.at[side, sub], own_sem)
    own.start()

    pad = jnp.full((LANES - slots - 8, rows), -1, jnp.int32)
    table = jnp.concatenate([src_t[...], jnp.broadcast_to(owner[...], (8, rows)), pad], axis=0)
    pair_start = (seg - side) * group_rows
    table = jnp.where(table < 0, -(1 << 28), table - pair_start)
    table = table.T
    for j in range(slots + 1):
        index[j] = jnp.broadcast_to(table[:, j : j + 1], (rows, LANES))

    from_x(0).wait_recv()
    for step in range(1, n_high):
        go(xy(step))

    @pl.when(has_target)
    def _():
        z(0, 0).start()

    for step in range(1, n_high):
        from_y(step, 1).wait_recv()
        go(yx(n_high - step))
    from_x(1).wait_recv()

    @pl.when(has_target)
    def _():
        z(0, 1).start()

    go(to_sibling(0, 1))
    for step in range(1, n_high):
        from_y(step, 0).wait_recv()
        go(to_sibling(n_high - step, 0))

    ops_copy.wait()

    def split_ops(start, stop):
        @pl.loop(start, stop)
        def _(j):
            ops_high[j], ops_low[j] = split(ops[j])

    split_ops(0, slots // 2)

    for step in range(1, n_high):
        from_xy(step).wait_recv()

        @pl.when(has_target)
        def _():
            z(n_high - step, 0).start()

    for step in range(1, n_high):
        from_yx(step).wait_recv()

        @pl.when(has_target)
        def _():
            z(step, 1).start()

        go(to_sibling(step, 1))

    split_ops(slots // 2, slots)

    own.wait()
    for step in range(n_high):
        from_sibling(step, 0).wait_recv()
    for step in range(n_high):
        from_sibling(step, 1).wait_recv()

    lane = lax.broadcasted_iota(jnp.int32, (1, LANES), 1)

    def one_hot(chosen, count, base):
        tiles = []
        for t in range(count // LANES):
            hit = chosen == lane + (base + t * LANES)
            tiles.append(jnp.where(hit, 1.0, 0.0).astype(jnp.bfloat16))
        return jnp.concatenate(tiles, axis=1)

    for s in range(2):
        for k in range(n_sub):
            at = pl.ds((s * n_sub + k) * rows, rows)
            pair_parts[at, :width], pair_parts[at, width:] = split(pair[s, k])

    chosen = index[slots]
    got = jnp.dot(one_hot(chosen, 2 * group_rows, 0), pair_parts[...], preferred_element_type=jnp.float32)
    owned_out[...] = got[:, :width] + got[:, width:]

    def near(start, stop):
        @pl.loop(start, stop)
        def _(b):
            chosen = index[pl.ds(b * BATCH, BATCH)].reshape(BATCH * rows, LANES)
            got = jnp.dot(
                one_hot(chosen, 2 * group_rows, 0), pair_parts[...], preferred_element_type=jnp.float32
            )
            picked[b] = got.astype(jnp.bfloat16)

    batches = slots // BATCH
    near(0, batches // 2)

    @pl.when(has_origin)
    def _():
        for step in range(n_high):
            for part in range(2):
                z(step, part).wait_recv()
            to_sibling(step, 2).start()

    near(batches // 2, batches)

    @pl.when(has_origin)
    def _():
        for step in range(n_high):
            from_sibling(step, 2).wait_recv()
        for k in range(n_sub):
            at = pl.ds(k * rows, rows)
            far_parts[at, :width], far_parts[at, width:] = split(far[k])

    far_base = -group_rows + side * (3 * group_rows)
    local_out[...] = jnp.zeros_like(local_out)

    def translate(with_far):
        @pl.loop(0, batches)
        def _(b):
            got = picked[b]
            if with_far:
                chosen = index[pl.ds(b * BATCH, BATCH)].reshape(BATCH * rows, LANES)
                more = jnp.dot(
                    one_hot(chosen, group_rows, far_base), far_parts[...], preferred_element_type=jnp.float32
                )
                got = got + more.astype(jnp.bfloat16)
            total = local_out[...]
            for i in range(BATCH):
                mine = got[i * rows : (i + 1) * rows]
                first, second = mine[:, :width], mine[:, width:]
                both = jnp.concatenate([first, second], axis=0)
                out = jnp.dot(both, ops_high[b * BATCH + i], preferred_element_type=jnp.float32)
                total = total + out[:rows] + out[rows:]
                total = total + jnp.dot(first, ops_low[b * BATCH + i], preferred_element_type=jnp.float32)
            local_out[...] = total

    @pl.when(has_origin)
    def _():
        translate(True)

    @pl.when(jnp.logical_not(has_origin))
    def _():
        translate(False)

    for c in sent:
        c.wait_send()

    @pl.when(has_target)
    def _():
        for step in range(n_high):
            for part in range(2):
                z(step, part).wait_send()

    @pl.when(has_origin)
    def _():
        for step in range(n_high):
            to_sibling(step, 2).wait_send()


def on_device(n_seg, n_sub, leaf_mult, m2m_ops, m2l_ops, owner_box, src_list):
    rows, width = leaf_mult.shape[0] // 8, leaf_mult.shape[1]
    slots = src_list.shape[1]
    children = leaf_mult.reshape(rows, 8, width)
    parent_mult = jnp.einsum("pck,ckl->pl", children, m2m_ops, precision=lax.Precision.HIGHEST)
    n_high = n_sub // 2
    messages = 2 + 4 * (n_high - 1) + 2 * n_high + 3 * n_high
    group_rows = rows * n_sub
    vmem = pl.BlockSpec(memory_space=pltpu.VMEM)
    half_type = jnp.bfloat16
    owned_mult, local_exp = pl.pallas_call(
        functools.partial(kernel, n_seg, n_sub),
        out_shape=[jax.ShapeDtypeStruct((rows, width), jnp.float32)] * 2,
        in_specs=[vmem, vmem, vmem, pl.BlockSpec(memory_space=pl.ANY)],
        out_specs=[vmem, vmem],
        scratch_shapes=[
            pltpu.VMEM((2, n_sub, rows, width), jnp.float32),
            pltpu.VMEM((n_sub, rows, width), jnp.float32),
            pltpu.VMEM((2 * group_rows, 2 * width), half_type),
            pltpu.VMEM((group_rows, 2 * width), half_type),
            pltpu.VMEM(m2l_ops.shape, jnp.float32),
            pltpu.VMEM(m2l_ops.shape, half_type),
            pltpu.VMEM(m2l_ops.shape, half_type),
            pltpu.VMEM((slots + 1, rows, LANES), jnp.int32),
            pltpu.VMEM((slots // BATCH, BATCH * rows, 2 * width), half_type),
            pltpu.SemaphoreType.DMA,
            pltpu.SemaphoreType.DMA,
            pltpu.SemaphoreType.DMA((messages,)),
            pltpu.SemaphoreType.DMA((messages,)),
        ],
        compiler_params=pltpu.CompilerParams(
            collective_id=0, has_side_effects=True, vmem_limit_bytes=60 << 20
        ),
    )(parent_mult, src_list.T, owner_box.reshape(1, rows), m2l_ops)
    return (parent_mult, owned_mult, local_exp)


def solution(mesh):
    n_seg, n_sub = mesh.shape["seg"], mesh.shape["sub"]
    in_specs = (P(("seg", "sub"), None), P(), P(), P(("seg", "sub")), P(("seg", "sub"), None))
    out_specs = (P(("seg", "sub"), None), P(("seg", "sub"), None), P(("seg", "sub"), None))
    return jax.shard_map(
        functools.partial(on_device, n_seg, n_sub),
        mesh=mesh, in_specs=in_specs, out_specs=out_specs, check_vma=False,
    )
```

time: 72.8 us -> 35.9 us (0.49)
  the two profiles are of different devices: /device:TPU:0 before, /device:TPU:17 now
where the time goes in v1:
time: 35.9 us; the launch traced here: 35.7 us
  Pallas kernels  27.1 us (75%)
  local copies, waits for them, and re-layouts  4.72 us (13%)
  matrix products  3.15 us (9%)
  between operations  0.65 us (2%)
    pallas_call x1, Pallas kernels, on_device(): pl.pallas_call(functools.partial(kernel, n_seg, n_sub), out_shape=[jax.Sh...  27.1 us
    unnamed x4, local copies, waits for them, and re-layouts  4.72 us
    dot_general x1, matrix products, on_device(): jnp.einsum('pck,ckl->pl', children, m2m_ops, precision=lax.Precision.HIGH...  3.15 us

profile of v1, /device:TPU:17, one launch (start us, length us, event | category | flops | bytes accessed | tf_op | source)
XLA Modules:
  0.0 35.7 jit_solution(17066967044098527474)
XLA Ops:
  0.6 0.0 copy-start
  0.6 1.6 %copy-done = f32[8,256,256]{2,1,0:T(8,128)S(1)} copy-done((f32[8,256,256]{2,1,0:T(8,128)S(1)}, f32[8,256,256]{2,1,0:T(8,128)}, u32[]{:S(2)}) %copy-start) | copy-done | bytes 2097176
  2.2 3.2 %convolution_bitcast_fusion.parent = f32[128,256]{1,0:T(8,128)} fusion(f32[8,256,256]{2,1,0:T(8,128)S(1)} %copy-done, f32[128,8,256]{2,1,0:T(8,128)} %bitcast.6), kind=kOutput, calls=%fused_computation | convolution fusion | flops 805306368 | bytes 3276800 | tf_op jit(solution)/shard_map/pck,ckl->pl/dot_general | solution.py:301
  5.4 27.1 %shard_map.76 = (f32[128,256]{1,0:T(8,128)}, f32[128,256]{1,0:T(8,128)}) custom-call(f32[128,256]{1,0:T(8,128)} %convolution_bitcast_fusion.parent, s32[32,128]{1,0:T(8,128)} %bitcast.7, s32[1,128]{1,0:T(1,128)} %bitcast.8, f32[32,256,256]{2,1,0:T(8,128)} %ops_hbm.1), custom_call_target="tpu_custom_call" | custom-call | tf_op jit(solution)/shard_map/pallas_call | solution.py:307
  32.5 1.6 %copy.13 = f32[128,256]{1,0:T(8,128)} copy(f32[128,256]{1,0:T(8,128)} %get-tuple-element.11) | data formatting | bytes 262144
  34.1 1.6 %copy.14 = f32[128,256]{1,0:T(8,128)} copy(f32[128,256]{1,0:T(8,128)} %get-tuple-element.12) | data formatting | bytes 262144
Async XLA Ops:
  0.6 1.6 %copy-start = (f32[8,256,256]{2,1,0:T(8,128)S(1)}, f32[8,256,256]{2,1,0:T(8,128)}, u32[]{:S(2)}) copy-start(f32[8,256,256]{2,1,0:T(8,128)} %param.6) | copy-start | bytes 6291460

commit v2 on v1

--- a/solution.py
+++ b/solution.py
@@ -19,9 +19,10 @@
 
 
 def kernel(
-    n_seg, n_sub, parent, src_t, owner, ops_hbm, owned_out, local_out,
+    n_seg, n_sub, leaf_hbm, up_hbm, src_t, owner, ops_hbm, sums,
+    leaf, up, parent,
     pair, far, pair_parts, far_parts, ops, ops_high, ops_low, index, picked,
-    ops_sem, own_sem, send_sem, recv_sem,
+    ops_sem, leaf_sem, up_sem, send_sem, recv_sem,
 ):
     seg, sub = lax.axis_index("seg"), lax.axis_index("sub")
     rows, width = parent.shape
@@ -38,6 +39,16 @@
     half = rows // 2
     group_rows = rows * n_sub
 
+    n_up = up.shape[0]
+    leaf_copies = [
+        pltpu.make_async_copy(leaf_hbm.at[:, pl.ds(t * LANES, LANES)], leaf.at[t], leaf_sem.at[t])
+        for t in range(width // LANES)
+    ]
+    for c in leaf_copies:
+        c.start()
+    up_copies = [pltpu.make_async_copy(up_hbm.at[c], up.at[c], up_sem.at[c]) for c in range(n_up)]
+    for c in up_copies:
+        c.start()
     ops_copy = pltpu.make_async_copy(ops_hbm, ops, ops_sem)
     ops_copy.start()
 
@@ -61,82 +72,6 @@
     @pl.when(has_origin)
     def _():
         greet(origin, sub)
-
-    pl.semaphore_wait(barrier, 1 + n_high + has_target.astype(jnp.int32) + has_origin.astype(jnp.int32))
-
-    names = {}
-
-    def copy(name, src, dst, to_seg, to_sub):
-        k = names.setdefault(name, len(names))
-        return pltpu.make_async_remote_copy(
-            src_ref=src, dst_ref=dst, send_sem=send_sem.at[k], recv_sem=recv_sem.at[k],
-            device_id=(to_seg, to_sub), device_id_type=MESH,
-        )
-
-    def piece(part):
-        return pl.ds(part * half, half)
-
-    sent = []
-
-    def go(c):
-        c.start()
-        sent.append(c)
-        return c
-
-    def to_x(part):
-        return copy(("x", part), parent.at[piece(part)], pair.at[side, sub, piece(part)], partner, sub)
-
-    def from_x(part):
-        return copy(("x", part), parent.at[piece(part)], pair.at[other_side, sub, piece(part)], partner, sub)
-
-    def to_y(step, part):
-        return copy(("y", step, part), parent.at[piece(part)], pair.at[side, sub, piece(part)], seg, peer(step))
-
-    def from_y(step, part):
-        at = pair.at[side, peer(n_high - step), piece(part)]
-        return copy(("y", step, part), parent.at[piece(part)], at, seg, peer(step))
-
-    def xy(step):
-        at = pair.at[other_side, sub, piece(0)]
-        return copy(("xy", step), at, at, seg, peer(step))
-
-    def from_xy(step):
-        at = pair.at[other_side, peer(n_high - step), piece(0)]
-        return copy(("xy", step), at, at, seg, peer(step))
-
-    def yx(step):
-        at = pair.at[side, peer(step), piece(1)]
-        return copy(("yx", step), at, at, partner, sub)
-
-    def from_yx(step):
-        at = pair.at[other_side, peer(step), piece(1)]
-        return copy(("yx", step), at, at, partner, sub)
-
-    def z(step, part):
-        return copy(
-            ("z", step, part), pair.at[other_side, peer(step), piece(part)],
-            far.at[peer(step), piece(part)], target, sub,
-        )
-
-    def to_sibling(step, which):
-        at = far.at[peer(step)] if which == 2 else pair.at[(side, other_side)[which], peer(step)]
-        src = parent if (step, which) == (0, 0) else at
-        return copy(("s", step, which), src, at, seg, sibling)
-
-    def from_sibling(step, which):
-        s = lax.rem(high + step, n_high) * 2 + 1 - core
-        at = far.at[s] if which == 2 else pair.at[(side, other_side)[which], s]
-        return copy(("s", step, which), at, at, seg, sibling)
-
-    go(to_x(0))
-    for step in range(1, n_high):
-        go(to_y(step, 1))
-    go(to_x(1))
-    for step in range(1, n_high):
-        go(to_y(step, 0))
-    go(to_sibling(0, 0))
-    own = pltpu.make_async_copy(parent, pair.at[side, sub], own_sem)
-    own.start()
 
     pad = jnp.full((LANES - slots - 8, rows), -1, jnp.int32)
     table = jnp.concatenate([src_t[...], jnp.broadcast_to(owner[...], (8, rows)), pad], axis=0)
@@ -146,6 +81,98 @@
     for j in range(slots + 1):
         index[j] = jnp.broadcast_to(table[:, j : j + 1], (rows, LANES))
 
+    def three_products(first, second, ops_first, ops_second):
+        both = jnp.concatenate([first, second], axis=0)
+        out = jnp.dot(both, ops_first, preferred_element_type=jnp.float32)
+        return out[:rows] + out[rows:] + jnp.dot(first, ops_second, preferred_element_type=jnp.float32)
+
+    for c in leaf_copies:
+        c.wait()
+    total = jnp.zeros((rows, width), jnp.float32)
+    for c in range(n_up):
+        up_copies[c].wait()
+        child = jnp.concatenate(
+            [leaf[t, pl.ds(c, rows, stride=n_up), :] for t in range(width // LANES)], axis=1
+        )
+        total = total + three_products(*split(child), *split(up[c]))
+    parent[...] = total
+
+    pl.semaphore_wait(barrier, 1 + n_high + has_target.astype(jnp.int32) + has_origin.astype(jnp.int32))
+
+    names = {}
+
+    def copy(name, src, dst, to_seg, to_sub):
+        k = names.setdefault(name, len(names))
+        return pltpu.make_async_remote_copy(
+            src_ref=src, dst_ref=dst, send_sem=send_sem.at[k], recv_sem=recv_sem.at[k],
+            device_id=(to_seg, to_sub), device_id_type=MESH,
+        )
+
+    def piece(part):
+        return pl.ds(part * half, half)
+
+    sent = []
+
+    def go(c):
+        c.start()
+        sent.append(c)
+        return c
+
+    def to_x(part):
+        return copy(("x", part), parent.at[piece(part)], pair.at[side, sub, piece(part)], partner, sub)
+
+    def from_x(part):
+        return copy(("x", part), parent.at[piece(part)], pair.at[other_side, sub, piece(part)], partner, sub)
+
+    def to_y(step, part):
+        return copy(("y", step, part), parent.at[piece(part)], pair.at[side, sub, piece(part)], seg, peer(step))
+
+    def from_y(step, part):
+        at = pair.at[side, peer(n_high - step), piece(part)]
+        return copy(("y", step, part), parent.at[piece(part)], at, seg, peer(step))
+
+    def xy(step):
+        at = pair.at[other_side, sub, piece(0)]
+        return copy(("xy", step), at, at, seg, peer(step))
+
+    def from_xy(step):
+        at = pair.at[other_side, peer(n_high - step), piece(0)]
+        return copy(("xy", step), at, at, seg, peer(step))
+
+    def yx(step):
+        at = pair.at[side, peer(step), piece(1)]
+        return copy(("yx", step), at, at, partner, sub)
+
+    def from_yx(step):
+        at = pair.at[other_side, peer(step), piece(1)]
+        return copy(("yx", step), at, at, partner, sub)
+
+    def z(step, part):
+        return copy(
+            ("z", step, part), pair.at[other_side, peer(step), piece(part)],
+            far.at[peer(step), piece(part)], target, sub,
+        )
+
+    def to_sibling(step, which):
+        at = far.at[peer(step)] if which == 2 else pair.at[(side, other_side)[which], peer(step)]
+        src = parent if (step, which) == (0, 0) else at
+        return copy(("s", step, which), src, at, seg, sibling)
+
+    def from_sibling(step, which):
+        s = lax.rem(high + step, n_high) * 2 + 1 - core
+        at = far.at[s] if which == 2 else pair.at[(side, other_side)[which], s]
+        return copy(("s", step, which), at, at, seg, sibling)
+
+    go(to_x(0))
+    for step in range(1, n_high):
+        go(to_y(step, 1))
+    go(to_x(1))
+    for step in range(1, n_high):
+        go(to_y(step, 0))
+    go(to_sibling(0, 0))
+    pair[side, sub] = parent[...]
+    sums[0] = parent[...]
+
     from_x(0).wait_recv()
     for step in range(1, n_high):
         go(xy(step))
@@ -195,7 +222,6 @@
 
     split_ops(slots // 2, slots)
 
-    own.wait()
     for step in range(n_high):
         from_sibling(step, 0).wait_recv()
     for step in range(n_high):
@@ -217,7 +243,8 @@
 
     chosen = index[slots]
     got = jnp.dot(one_hot(chosen, 2 * group_rows, 0), pair_parts[...], preferred_element_type=jnp.float32)
-    owned_out[...] = got[:, :width] + got[:, width:]
+    sums[1] = got[:, :width]
+    sums[2] = got[:, width:]
 
     def near(start, stop):
         @pl.loop(start, stop)
@@ -249,7 +276,8 @@
             far_parts[at, :width], far_parts[at, width:] = split(far[k])
 
     far_base = -group_rows + side * (3 * group_rows)
-    local_out[...] = jnp.zeros_like(local_out)
+    sums[3] = jnp.zeros((rows, width), jnp.float32)
+    sums[4] = jnp.zeros((rows, width), jnp.float32)
 
     def translate(with_far):
         @pl.loop(0, batches)
@@ -261,15 +289,16 @@
                     one_hot(chosen, group_rows, far_base), far_parts[...], preferred_element_type=jnp.float32
                 )
                 got = got + more.astype(jnp.bfloat16)
-            total = local_out[...]
+            total, rest = sums[3], sums[4]
             for i in range(BATCH):
                 mine = got[i * rows : (i + 1) * rows]
                 first, second = mine[:, :width], mine[:, width:]
                 both = jnp.concatenate([first, second], axis=0)
                 out = jnp.dot(both, ops_high[b * BATCH + i], preferred_element_type=jnp.float32)
-                total = total + out[:rows] + out[rows:]
-                total = total + jnp.dot(first, ops_low[b * BATCH + i], preferred_element_type=jnp.float32)
-            local_out[...] = total
+                total = total + out[:rows]
+                rest = rest + out[rows:]
+                rest = rest + jnp.dot(first, ops_low[b * BATCH + i], preferred_element_type=jnp.float32)
+            sums[3], sums[4] = total, rest
 
     @pl.when(has_origin)
     def _():
@@ -297,19 +326,21 @@
 def on_device(n_seg, n_sub, leaf_mult, m2m_ops, m2l_ops, owner_box, src_list):
     rows, width = leaf_mult.shape[0] // 8, leaf_mult.shape[1]
     slots = src_list.shape[1]
-    children = leaf_mult.reshape(rows, 8, width)
-    parent_mult = jnp.einsum("pck,ckl->pl", children, m2m_ops, precision=lax.Precision.HIGHEST)
     n_high = n_sub // 2
     messages = 2 + 4 * (n_high - 1) + 2 * n_high + 3 * n_high
     group_rows = rows * n_sub
     vmem = pl.BlockSpec(memory_space=pltpu.VMEM)
+    hbm = pl.BlockSpec(memory_space=pl.ANY)
     half_type = jnp.bfloat16
-    owned_mult, local_exp = pl.pallas_call(
+    sums = pl.pallas_call(
         functools.partial(kernel, n_seg, n_sub),
-        out_shape=[jax.ShapeDtypeStruct((rows, width), jnp.float32)] * 2,
-        in_specs=[vmem, vmem, vmem, pl.BlockSpec(memory_space=pl.ANY)],
-        out_specs=[vmem, vmem],
+        out_shape=jax.ShapeDtypeStruct((5, rows, width), jnp.float32),
+        in_specs=[hbm, hbm, vmem, vmem, hbm],
+        out_specs=vmem,
         scratch_shapes=[
+            pltpu.VMEM((width // LANES, leaf_mult.shape[0], LANES), jnp.float32),
+            pltpu.VMEM(m2m_ops.shape, jnp.float32),
+            pltpu.VMEM((rows, width), jnp.float32),
             pltpu.VMEM((2, n_sub, rows, width), jnp.float32),
             pltpu.VMEM((n_sub, rows, width), jnp.float32),
             pltpu.VMEM((2 * group_rows, 2 * width), half_type),
@@ -320,15 +351,16 @@
             pltpu.VMEM((slots + 1, rows, LANES), jnp.int32),
             pltpu.VMEM((slots // BATCH, BATCH * rows, 2 * width), half_type),
             pltpu.SemaphoreType.DMA,
-            pltpu.SemaphoreType.DMA,
+            pltpu.SemaphoreType.DMA((width // LANES,)),
+            pltpu.SemaphoreType.DMA((m2m_ops.shape[0],)),
             pltpu.SemaphoreType.DMA((messages,)),
             pltpu.SemaphoreType.DMA((messages,)),
         ],
         compiler_params=pltpu.CompilerParams(
             collective_id=0, has_side_effects=True, vmem_limit_bytes=60 << 20
         ),
-    )(parent_mult, src_list.T, owner_box.reshape(1, rows), m2l_ops)
-    return (parent_mult, owned_mult, local_exp)
+    )(leaf_mult, m2m_ops, src_list.T, owner_box.reshape(1, rows), m2l_ops)
+    return (sums[0], sums[1] + sums[2], sums[3] + sums[4])
 
 
 def solution(mesh):

time: 35.9 us -> 32.2 us (0.90)
  local copies, waits for them, and re-layouts: 4.72 us -> 0 us
  matrix products: 3.15 us -> 0 us
  Pallas kernels: 27.1 us -> 29.3 us
  other arithmetic: 0 us -> 1.92 us
    unnamed x4 -> x0, local copies, waits for them, and re-layouts: 4.72 us -> none
    dot_general x1 -> x0, matrix products: 3.15 us -> none  [on_device(): jnp.einsum('pck,ckl->pl', children, m2m_ops, precision=lax.Precision.HIGH...]
    pallas_call x1, Pallas kernels: 27.1 us -> 29.3 us  [on_device(): pl.pallas_call(functools.partial(kernel, n_seg, n_sub), out_shape=jax.Sha...]
    add x0 -> x1, other arithmetic: none -> 1.92 us  [on_device(): return (sums[0], sums[1] + sums[2], sums[3] + sums[4])]
where the time goes in v2:
time: 32.2 us; the launch traced here: 31.9 us
  Pallas kernels  29.3 us (91%)
  other arithmetic  1.92 us (6%)
  between operations  0.64 us (2%)
    pallas_call x1, Pallas kernels, on_device(): pl.pallas_call(functools.partial(kernel, n_seg, n_sub), out_shape=jax.Sha...  29.3 us
    add x1, other arithmetic, on_device(): return (sums[0], sums[1] + sums[2], sums[3] + sums[4])  1.92 us

profile of v2, /device:TPU:17, one launch (start us, length us, event | category | flops | bytes accessed | tf_op | source)
XLA Modules:
  0.0 31.9 jit_solution(5554645847609209934)
XLA Ops:
  0.6 29.3 %shard_map.76 = f32[5,128,256]{2,1,0:T(8,128)} custom-call(f32[1024,256]{1,0:T(8,128)} %leaf_hbm.1, f32[8,256,256]{2,1,0:T(8,128)} %up_hbm.1, s32[32,128]{1,0:T(8,128)} %bitcast.8, s32[1,128]{1,0:T(1,128)} %bitcast.9, f32[32,256,256]{2,1,0:T(8,128)} %ops_hbm.1), custom_call_target="tpu_custom_call" | custom-call | tf_op jit(solution)/shard_map/pallas_call | solution.py:335
  30.0 1.9 %add_bitcast_fusion = (f32[128,256]{1,0:T(8,128)}, f32[128,256]{1,0:T(8,128)}, f32[128,256]{1,0:T(8,128)}) fusion(f32[5,128,256]{2,1,0:T(8,128)} %shard_map.76), kind=kLoop, calls=%fused_computation | loop fusion | flops 65536 | bytes 1048576 | tf_op jit(solution)/shard_map/add | solution.py:363

commit v3 on v2

--- a/solution.py
+++ b/solution.py
@@ -49,8 +49,11 @@
     up_copies = [pltpu.make_async_copy(up_hbm.at[c], up.at[c], up_sem.at[c]) for c in range(n_up)]
     for c in up_copies:
         c.start()
-    ops_copy = pltpu.make_async_copy(ops_hbm, ops, ops_sem)
-    ops_copy.start()
+    middle = slots // 2
+    ops_copies = [
+        pltpu.make_async_copy(ops_hbm.at[at], ops.at[at], ops_sem.at[k])
+        for k, at in enumerate((pl.ds(0, middle), pl.ds(middle, slots - middle)))
+    ]
 
     barrier = pltpu.get_barrier_semaphore()
 
@@ -91,6 +94,9 @@
     total = jnp.zeros((rows, width), jnp.float32)
     for c in range(n_up):
         up_copies[c].wait()
+        if c == n_up // 2:
+            for one in ops_copies:
+                one.start()
         child = jnp.concatenate(
             [leaf[t, pl.ds(c, rows, stride=n_up), :] for t in range(width // LANES)], axis=1
         )
@@ -173,36 +179,35 @@
     pair[side, sub] = parent[...]
     sums[0] = parent[...]
 
-    from_x(0).wait_recv()
-    for step in range(1, n_high):
-        go(xy(step))
-
-    @pl.when(has_target)
-    def _():
-        z(0, 0).start()
-
-    for step in range(1, n_high):
-        from_y(step, 1).wait_recv()
-        go(yx(n_high - step))
-    from_x(1).wait_recv()
-
-    @pl.when(has_target)
-    def _():
-        z(0, 1).start()
-
-    go(to_sibling(0, 1))
-    for step in range(1, n_high):
-        from_y(step, 0).wait_recv()
-        go(to_sibling(n_high - step, 0))
-
-    ops_copy.wait()
-
     def split_ops(start, stop):
         @pl.loop(start, stop)
         def _(j):
             ops_high[j], ops_low[j] = split(ops[j])
 
-    split_ops(0, slots // 2)
+    ops_copies[0].wait()
+    split_ops(0, middle)
+
+    from_x(0).wait_recv()
+    for step in range(1, n_high):
+        go(xy(step))
+
+    @pl.when(has_target)
+    def _():
+        z(0, 0).start()
+
+    for step in range(1, n_high):
+        from_y(step, 1).wait_recv()
+        go(yx(n_high - step))
+    from_x(1).wait_recv()
+
+    @pl.when(has_target)
+    def _():
+        z(0, 1).start()
+
+    go(to_sibling(0, 1))
+    for step in range(1, n_high):
+        from_y(step, 0).wait_recv()
+        go(to_sibling(n_high - step, 0))
 
     for step in range(1, n_high):
         from_xy(step).wait_recv()
@@ -220,7 +225,9 @@
 
         go(to_sibling(step, 1))
 
-    split_ops(slots // 2, slots)
+
+    ops_copies[1].wait()
+    split_ops(middle, slots)
 
     for step in range(n_high):
         from_sibling(step, 0).wait_recv()
@@ -350,7 +357,7 @@
             pltpu.VMEM(m2l_ops.shape, half_type),
             pltpu.VMEM((slots + 1, rows, LANES), jnp.int32),
             pltpu.VMEM((slots // BATCH, BATCH * rows, 2 * width), half_type),
-            pltpu.SemaphoreType.DMA,
+            pltpu.SemaphoreType.DMA((2,)),
             pltpu.SemaphoreType.DMA((width // LANES,)),
             pltpu.SemaphoreType.DMA((m2m_ops.shape[0],)),
             pltpu.SemaphoreType.DMA((messages,)),

time: 32.2 us -> 32 us (level)
  no operation moved by 1% of the time
where the time goes in v3:
time: 32 us; the launch traced here: 31.8 us
  Pallas kernels  29.2 us (91%)
  other arithmetic  1.92 us (6%)
  between operations  0.64 us (2%)
    pallas_call x1, Pallas kernels, on_device(): pl.pallas_call(functools.partial(kernel, n_seg, n_sub), out_shape=jax.Sha...  29.2 us
    add x1, other arithmetic, on_device(): return (sums[0], sums[1] + sums[2], sums[3] + sums[4])  1.92 us

profile of v3, /device:TPU:17, one launch (start us, length us, event | category | flops | bytes accessed | tf_op | source)
XLA Modules:
  0.0 31.8 jit_solution(347017338314164941)
XLA Ops:
  0.6 29.2 %shard_map.76 = f32[5,128,256]{2,1,0:T(8,128)} custom-call(f32[1024,256]{1,0:T(8,128)} %leaf_hbm.1, f32[8,256,256]{2,1,0:T(8,128)} %up_hbm.1, s32[32,128]{1,0:T(8,128)} %bitcast.8, s32[1,128]{1,0:T(1,128)} %bitcast.9, f32[32,256,256]{2,1,0:T(8,128)} %ops_hbm.1), custom_call_target="tpu_custom_call" | custom-call | tf_op jit(solution)/shard_map/pallas_call | solution.py:342
  29.8 1.9 %add_bitcast_fusion = (f32[128,256]{1,0:T(8,128)}, f32[128,256]{1,0:T(8,128)}, f32[128,256]{1,0:T(8,128)}) fusion(f32[5,128,256]{2,1,0:T(8,128)} %shard_map.76), kind=kLoop, calls=%fused_computation | loop fusion | flops 65536 | bytes 1048576 | tf_op jit(solution)/shard_map/add | solution.py:370

commit v4 on v3

--- a/solution.py
+++ b/solution.py
@@ -9,7 +9,8 @@
 
 MESH = pl.DeviceIdType.MESH
 LANES = 128
-BATCH = 4
+BATCH = 16
+PARTS = 4
 
 
 def split(value):
@@ -36,7 +37,7 @@
     origin = seg - 2 + 4 * side
     has_target = (target >= 0) & (target < n_seg)
     has_origin = (origin >= 0) & (origin < n_seg)
-    half = rows // 2
+    half = rows // PARTS
     group_rows = rows * n_sub
 
     n_up = up.shape[0]
@@ -137,21 +138,21 @@
         at = pair.at[side, peer(n_high - step), piece(part)]
         return copy(("y", step, part), parent.at[piece(part)], at, seg, peer(step))
 
-    def xy(step):
-        at = pair.at[other_side, sub, piece(0)]
-        return copy(("xy", step), at, at, seg, peer(step))
-
-    def from_xy(step):
-        at = pair.at[other_side, peer(n_high - step), piece(0)]
-        return copy(("xy", step), at, at, seg, peer(step))
-
-    def yx(step):
-        at = pair.at[side, peer(step), piece(1)]
-        return copy(("yx", step), at, at, partner, sub)
-
-    def from_yx(step):
-        at = pair.at[other_side, peer(step), piece(1)]
-        return copy(("yx", step), at, at, partner, sub)
+    def xy(step, part):
+        at = pair.at[other_side, sub, piece(part)]
+        return copy(("xy", step, part), at, at, seg, peer(step))
+
+    def from_xy(step, part):
+        at = pair.at[other_side, peer(n_high - step), piece(part)]
+        return copy(("xy", step, part), at, at, seg, peer(step))
+
+    def yx(step, part):
+        at = pair.at[side, peer(step), piece(part)]
+        return copy(("yx", step, part), at, at, partner, sub)
+
+    def from_yx(step, part):
+        at = pair.at[other_side, peer(step), piece(part)]
+        return copy(("yx", step, part), at, at, partner, sub)
 
     def z(step, part):
         return copy(
@@ -169,12 +170,10 @@
         at = far.at[s] if which == 2 else pair.at[(side, other_side)[which], s]
         return copy(("s", step, which), at, at, seg, sibling)
 
-    go(to_x(0))
-    for step in range(1, n_high):
-        go(to_y(step, 1))
-    go(to_x(1))
-    for step in range(1, n_high):
-        go(to_y(step, 0))
+    for part in range(PARTS):
+        go(to_x(part))
+        for step in range(1, n_high):
+            go(to_y(step, PARTS - 1 - part))
     go(to_sibling(0, 0))
     pair[side, sub] = parent[...]
     sums[0] = parent[...]
@@ -187,44 +186,41 @@
     ops_copies[0].wait()
     split_ops(0, middle)
 
-    from_x(0).wait_recv()
-    for step in range(1, n_high):
-        go(xy(step))
-
-    @pl.when(has_target)
-    def _():
-        z(0, 0).start()
-
-    for step in range(1, n_high):
-        from_y(step, 1).wait_recv()
-        go(yx(n_high - step))
-    from_x(1).wait_recv()
-
-    @pl.when(has_target)
-    def _():
-        z(0, 1).start()
+    for part in range(PARTS):
+        from_x(part).wait_recv()
+
+        @pl.when(has_target)
+        def _():
+            z(0, part).start()
+
+        for step in range(1, n_high):
+            if part < PARTS // 2:
+                go(xy(step, part))
+        for step in range(1, n_high):
+            from_y(step, PARTS - 1 - part).wait_recv()
+            if part < PARTS // 2:
+                go(yx(n_high - step, PARTS - 1 - part))
 
     go(to_sibling(0, 1))
     for step in range(1, n_high):
-        from_y(step, 0).wait_recv()
         go(to_sibling(n_high - step, 0))
 
+    for part in range(PARTS // 2):
+        for step in range(1, n_high):
+            from_xy(step, part).wait_recv()
+
+            @pl.when(has_target)
+            def _():
+                z(n_high - step, part).start()
+
+            from_yx(step, PARTS - 1 - part).wait_recv()
+
+            @pl.when(has_target)
+            def _():
+                z(step, PARTS - 1 - part).start()
+
     for step in range(1, n_high):
-        from_xy(step).wait_recv()
-
-        @pl.when(has_target)
-        def _():
-            z(n_high - step, 0).start()
-
-    for step in range(1, n_high):
-        from_yx(step).wait_recv()
-
-        @pl.when(has_target)
-        def _():
-            z(step, 1).start()
-
         go(to_sibling(step, 1))
-
 
     ops_copies[1].wait()
     split_ops(middle, slots)
@@ -249,7 +245,8 @@
             pair_parts[at, :width], pair_parts[at, width:] = split(pair[s, k])
 
     chosen = index[slots]
-    got = jnp.dot(one_hot(chosen, 2 * group_rows, 0), pair_parts[...], preferred_element_type=jnp.float32)
+    own_rows = pair_parts[pl.ds(pl.multiple_of(side * group_rows, LANES), group_rows), :]
+    got = jnp.dot(one_hot(chosen, group_rows, side * group_rows), own_rows, preferred_element_type=jnp.float32)
     sums[1] = got[:, :width]
     sums[2] = got[:, width:]
 
@@ -268,7 +265,7 @@
     @pl.when(has_origin)
     def _():
         for step in range(n_high):
-            for part in range(2):
+            for part in range(PARTS):
                 z(step, part).wait_recv()
             to_sibling(step, 2).start()
 
@@ -321,7 +318,7 @@
     @pl.when(has_target)
     def _():
         for step in range(n_high):
-            for part in range(2):
+            for part in range(PARTS):
                 z(step, part).wait_send()
 
     @pl.when(has_origin)
@@ -334,7 +331,7 @@
     rows, width = leaf_mult.shape[0] // 8, leaf_mult.shape[1]
     slots = src_list.shape[1]
     n_high = n_sub // 2
-    messages = 2 + 4 * (n_high - 1) + 2 * n_high + 3 * n_high
+    messages = PARTS * (3 * n_high - 1) + 3 * n_high
     group_rows = rows * n_sub
     vmem = pl.BlockSpec(memory_space=pltpu.VMEM)
     hbm = pl.BlockSpec(memory_space=pl.ANY)

time: 32 us -> 29.2 us (0.912)
  Pallas kernels: 29.2 us -> 26.4 us
    pallas_call x1, Pallas kernels: 29.2 us -> 26.4 us  [on_device(): pl.pallas_call(functools.partial(kernel, n_seg, n_sub), out_shape=jax.Sha...]
where the time goes in v4:
time: 29.2 us; the launch traced here: 29 us
  Pallas kernels  26.4 us (90%)
  other arithmetic  1.92 us (7%)
  between operations  0.64 us (2%)
    pallas_call x1, Pallas kernels, on_device(): pl.pallas_call(functools.partial(kernel, n_seg, n_sub), out_shape=jax.Sha...  26.4 us
    add x1, other arithmetic, on_device(): return (sums[0], sums[1] + sums[2], sums[3] + sums[4])  1.92 us

profile of v4, /device:TPU:17, one launch (start us, length us, event | category | flops | bytes accessed | tf_op | source)
XLA Modules:
  0.0 29.0 jit_solution(9053500842075132052)
XLA Ops:
  0.6 26.4 %shard_map.76 = f32[5,128,256]{2,1,0:T(8,128)} custom-call(f32[1024,256]{1,0:T(8,128)} %leaf_hbm.1, f32[8,256,256]{2,1,0:T(8,128)} %up_hbm.1, s32[32,128]{1,0:T(8,128)} %bitcast.8, s32[1,128]{1,0:T(1,128)} %bitcast.9, f32[32,256,256]{2,1,0:T(8,128)} %ops_hbm.1), custom_call_target="tpu_custom_call" | custom-call | tf_op jit(solution)/shard_map/pallas_call | solution.py:339
  27.0 1.9 %add_bitcast_fusion = (f32[128,256]{1,0:T(8,128)}, f32[128,256]{1,0:T(8,128)}, f32[128,256]{1,0:T(8,128)}) fusion(f32[5,128,256]{2,1,0:T(8,128)} %shard_map.76), kind=kLoop, calls=%fused_computation | loop fusion | flops 65536 | bytes 1048576 | tf_op jit(solution)/shard_map/add | solution.py:367
